TPU v7x, 32 devices: a whole 2x2x4 slice. The times are simulated.
32 devices in a mesh: tok: 8 (over y, x, core), col: 4 (over z).
Axes of the slice: x: 2, y: 2, z: 4, core: 2. Of those that a mesh axis runs over, the one named last changes fastest.
Arguments:
- activations: bfloat16 [2, 12288, 4096], P(None, 'tok', 'col'), may hold values from -6 to 6
- out_grads: bfloat16 [2, 12288, 4096], P(None, 'tok', 'col'), may hold values from -0.059814453 to 0.059814453
- token_mask: int32 [2, 12288], P(None, 'tok'), may hold values 0 or 1
- row_signs: int32 [4096], P('tok'), may hold values from 0 to 1
- col_signs: int32 [4096], P('col'), may hold values from 0 to 1
- bank: float32 [16, 4096, 4096], P(None, 'tok', 'col'), may hold values from -6 to 6
- bank_index: int32 [2], replicated, may hold values from 0 to 15, as said below
Outputs:
- fingerprints: float32 [2, 4096, 4096], P(None, 'tok', 'col')
- scores: float32 [2], replicated
Inputs may be any that keep to these rules, and one draw needn't show every extreme that they name: `bank_index`: the 2 values are distinct, and one of them is 15.
All inputs are finite; a program needn't handle non-finite values. No bound on the sum of `token_mask` on one device may be relied on, other than what follows from the above.
Results may differ from a plain program's by a relative error of at most 0.0003.
Values may be sent and summed in bfloat16 or wider, within the bound.
No kernel may reach another device: no remote copies, remote signals or barrier semaphores. Data moves between devices by JAX's collectives and lax.ppermute only.
A program may use at most 192 MiB of HBM per device.

v0:
```python
import math
import jax
import jax.numpy as jnp
from jax import lax
from jax.sharding import PartitionSpec as P

D = 4096
HIGH = lax.Precision.HIGHEST


def hadamard(order):
    positions = jnp.arange(order, dtype=jnp.int32)
    common_bits = jnp.bitwise_and(positions[:, None], positions[None, :])
    parity = jnp.zeros((order, order), jnp.int32)
    for bit_number in range(max(order.bit_length() - 1, 0)):
        parity = parity + jnp.bitwise_and(jnp.right_shift(common_bits, bit_number), 1)
    return (1 - 2 * (parity % 2)).astype(jnp.float32)


def body(activations, out_grads, token_mask, row_signs, col_signs, bank, bank_index):
    row_pm = (2 * row_signs - 1).astype(jnp.float32)
    col_pm = (2 * col_signs - 1).astype(jnp.float32)
    tok_count = lax.axis_size("tok")
    col_count = lax.axis_size("col")
    local_rows = row_pm.shape[0]
    local_cols = col_pm.shape[0]
    tok_table = hadamard(tok_count)
    col_table = hadamard(col_count)
    rows_table = hadamard(local_rows)
    cols_table = hadamard(local_cols)
    factor = 1.0 / math.sqrt(D)
    squared = float(D) * float(D)
    all_signs = lax.all_gather(row_signs, "tok", axis=0, tiled=True)
    full_pm = (2 * all_signs - 1).astype(jnp.float32)
    prints = []
    crosses = []
    owns = []
    refsqs = []
    for seq_number in range(activations.shape[0]):
        features = lax.all_gather(activations[seq_number], "col", axis=1, tiled=True)
        masked = out_grads[seq_number] * token_mask[seq_number][:, None].astype(jnp.bfloat16)
        partial_value = jnp.einsum(
            "tr,tc->rc", features, masked, preferred_element_type=jnp.float32
        )
        blocks = (partial_value * full_pm[:, None]).reshape(tok_count, local_rows, local_cols)
        blocks = jnp.einsum("rs,asc->arc", rows_table, blocks, precision=HIGH)
        blocks = jnp.einsum("ab,brc->arc", tok_table, blocks, precision=HIGH)
        premixed = blocks.reshape(tok_count * local_rows, local_cols)

        def term_rows(row_start, row_count, premixed=premixed):
            return premixed

        summed = lax.psum_scatter(
            term_rows(jnp.int32(0), lax.axis_size("tok") * local_rows),
            "tok",
            scatter_dimension=0,
            tiled=True,
        )
        slab = summed
        slab = slab * factor
        slab = jnp.dot(slab * col_pm[None, :], cols_table, precision=HIGH)
        pieces = slab.reshape(col_count, local_rows // col_count, local_cols)
        col_pieces = lax.all_to_all(pieces, "col", split_axis=0, concat_axis=0, tiled=True)
        mixed_cols = jnp.einsum("ab,brc->arc", col_table, col_pieces, precision=HIGH)
        pieces = lax.all_to_all(mixed_cols, "col", split_axis=0, concat_axis=0, tiled=True)
        slab = pieces.reshape(local_rows, local_cols)
        slab = slab * factor
        chosen = lax.dynamic_index_in_dim(bank, bank_index[seq_number], 0, keepdims=False)
        prints.append(slab)
        crosses.append(jnp.sum(slab * chosen))
        owns.append(jnp.sum(slab * slab))
        refsqs.append(jnp.sum(chosen * chosen))
    cross, own, refsq = lax.psum(
        (jnp.stack(crosses), jnp.stack(owns), jnp.stack(refsqs)), ("tok", "col")
    )
    scores = D * (cross / squared) / jnp.sqrt((own / squared + 1e-06) * (refsq / squared + 1e-06))
    return (jnp.stack(prints), scores)


def solution(mesh):
    in_specs = (
        P(None, "tok", "col"),
        P(None, "tok", "col"),
        P(None, "tok"),
        P("tok"),
        P("col"),
        P(None, "tok", "col"),
        P(),
    )
    out_specs = (P(None, "tok", "col"), P())
    return jax.shard_map(body, mesh=mesh, in_specs=in_specs, out_specs=out_specs, check_vma=False)
```

profile of v0, /device:TPU:10, one launch (start us, length us, event | category | flops | bytes accessed | tf_op | source)
XLA Modules:
  0.0 921.1 jit_solution(13478157805509062199)
XLA Ops:
  7.2 6.3 fusion.137
  14.3 8.9 all-gather.2
  23.3 206.9 %all-gather.8.cloned.1.call-done = bf16[1,1536,4096]{2,1,0:T(8,128)(2,1)} async-done(((bf16[1,1536,1024]{2,1,0:T(8,128)(2,1)}), bf16[1,1536,4096]{2,1,0:T(8,128)(2,1)}) %all-gather.8.cloned.1.call-update) | async-done | bytes 12582928 | tf_op jit(solution)/shard_map/all_gather | solution.py:40
  230.2 18.0 %fusion.7 = f32[1024,4096]{1,0:T(8,128)S(1)} fusion(bf16[1,1536,4096]{2,1,0:T(8,128)(2,1)} %all-gather.8.cloned.1.call-done, f32[4096]{0:T(1024)S(1)} %bitcast.90, bf16[2,1536,1024]{2,1,0:T(8,128)(2,1)} %param.8, bf16[1536]{0:T(1024)(128)(2,1)S(1)} %get-tuple-element.7), kind=kOutput, calls=%fused_computation.5 | convolution fusion | flops 12890669056 | bytes 32525312 | tf_op jit(solution)/shard_map/tr,tc->rc/dot_general | solution.py:42
  248.3 10.6 %copy.28 = f32[128,8,8,512]{3,2,1,0:T(8,128)S(1)} copy(f32[128,8,8,512]{3,1,2,0:T(8,128)S(1)} %bitcast.87) | data formatting | bytes 33554432
  258.9 34.4 %convolution_bitcast_fusion = f32[8,512,1024]{1,0,2:T(8,128)} fusion(f32[8,512,1024]{1,0,2:T(8,128)S(1)} %bitcast.80), kind=kOutput, calls=%fused_computation.6 | convolution fusion | flops 25780551680 | bytes 33554432 | tf_op jit(solution)/shard_map/rs,asc->arc/dot_general | solution.py:46
  293.3 16.7 %copy.23 = f32[8,512,1024]{2,0,1:T(8,128)} copy(f32[8,512,1024]{1,0,2:T(8,128)} %convolution_bitcast_fusion) | data formatting | bytes 33554432 | tf_op jit(solution)/shard_map/rs,asc->arc/transpose | solution.py:46
  310.0 21.6 %fusion.64 = f32[8,512,1024]{2,0,1:T(8,128)} fusion(f32[8,512,1024]{2,0,1:T(8,128)} %copy.23), kind=kOutput, calls=%fused_computation.82 | convolution fusion | flops 402654656 | bytes 33554432 | tf_op jit(solution)/shard_map/ab,brc->arc/dot_general | solution.py:47
  331.6 17.7 %copy.24 = f32[8,512,1024]{2,1,0:T(8,128)} copy(f32[8,512,1024]{2,0,1:T(8,128)} %fusion.64) | data formatting | bytes 33554432 | tf_op jit(solution)/shard_map/ab,brc->arc/dot_general | solution.py:47
  349.4 99.4 %all-gather.6.cloned.1.call-done = bf16[1,1536,4096]{2,1,0:T(8,128)(2,1)} async-done(((bf16[1,1536,1024]{2,1,0:T(8,128)(2,1)}), bf16[1,1536,4096]{2,1,0:T(8,128)(2,1)}) %all-gather.6.cloned.1.call-update) | async-done | bytes 12582928 | tf_op jit(solution)/shard_map/all_gather | solution.py:40
  448.8 18.4 %fusion.4 = f32[1024,4096]{1,0:T(8,128)S(1)} fusion(bf16[1,1536,4096]{2,1,0:T(8,128)(2,1)} %all-gather.6.cloned.1.call-done, f32[4096]{0:T(1024)S(1)} %bitcast.91, bf16[2,1536,1024]{2,1,0:T(8,128)(2,1)} %param.8, bf16[1536]{0:T(1024)(128)(2,1)S(1)} %get-tuple-element.6), kind=kOutput, calls=%fused_computation.4 | convolution fusion | flops 12890669056 | bytes 32525312 | tf_op jit(solution)/shard_map/tr,tc->rc/dot_general | solution.py:42
  467.2 10.6 %copy.27 = f32[128,8,8,512]{3,2,1,0:T(8,128)S(1)} copy(f32[128,8,8,512]{3,1,2,0:T(8,128)S(1)} %bitcast.86) | data formatting | bytes 33554432
  477.8 34.4 %convolution_bitcast_fusion.1 = f32[8,512,1024]{1,0,2:T(8,128)} fusion(f32[8,512,1024]{1,0,2:T(8,128)S(1)} %bitcast.81), kind=kOutput, calls=%fused_computation.7 | convolution fusion | flops 25780551680 | bytes 33554432 | tf_op jit(solution)/shard_map/rs,asc->arc/dot_general | solution.py:46
  512.2 17.0 %copy.19 = f32[8,512,1024]{2,0,1:T(8,128)} copy(f32[8,512,1024]{1,0,2:T(8,128)} %convolution_bitcast_fusion.1) | data formatting | bytes 33554432 | tf_op jit(solution)/shard_map/rs,asc->arc/transpose | solution.py:46
  529.2 21.6 %fusion.66 = f32[8,512,1024]{2,0,1:T(8,128)} fusion(f32[8,512,1024]{2,0,1:T(8,128)} %copy.19), kind=kOutput, calls=%fused_computation.83 | convolution fusion | flops 402654656 | bytes 33554432 | tf_op jit(solution)/shard_map/ab,brc->arc/dot_general | solution.py:47
  550.9 17.7 %copy.20 = f32[8,512,1024]{2,1,0:T(8,128)} copy(f32[8,512,1024]{2,0,1:T(8,128)} %fusion.66) | data formatting | bytes 33554432 | tf_op jit(solution)/shard_map/ab,brc->arc/dot_general | solution.py:47
  569.5 16.7 %fusion.24 = f32[512,1024]{1,0:T(8,128)} fusion(f32[512,1024]{1,0:T(8,128)} %reduce-scatter.5.cloned.1.call-done, f32[1024]{0:T(1024)S(1)} %convert_multiply_fusion), kind=kOutput, calls=%fused_computation.34 | convolution fusion | flops 6489112576 | bytes 4198400 | tf_op jit(solution)/shard_map/dot_general | solution.py:61
  586.2 6.9 all-to-all-start.2
  593.1 96.1 %reduce-scatter.3.cloned.1.call-done = f32[512,1024]{1,0:T(8,128)} async-done(((f32[4096,1024]{1,0:T(8,128)}), f32[512,1024]{1,0:T(8,128)}) %reduce-scatter.3.cloned.1.call-update) | async-done | bytes 2097168 | tf_op jit(solution)/shard_map/reduce_scatter | solution.py:53
  689.2 16.3 %fusion.27 = f32[512,1024]{1,0:T(8,128)} fusion(f32[512,1024]{1,0:T(8,128)} %reduce-scatter.3.cloned.1.call-done, f32[1024]{0:T(1024)S(1)} %convert_multiply_fusion), kind=kOutput, calls=%fused_computation.36 | convolution fusion | flops 6489112576 | bytes 4198400 | tf_op jit(solution)/shard_map/dot_general | solution.py:61
  705.5 5.1 all-to-all-start
  710.6 4.2 fusion.20
  717.4 38.1 %all-to-all-done = f32[4,128,1024]{2,1,0:T(8,128)} async-done(((f32[4,128,1024]{2,1,0:T(8,128)}), f32[4,128,1024]{2,1,0:T(8,128)}, u32[]{:S(2)}, u32[]{:S(2)}) %all-to-all-start) | async-done | bytes 2097184 | tf_op jit(solution)/shard_map/all_to_all | solution.py:63
  755.4 7.2 all-to-all-start.3
  762.6 6.5 fusion.22
  771.7 35.4 %all-to-all-done.3 = f32[4,128,1024]{2,1,0:T(8,128)S(1)} async-done(((f32[4,128,1024]{2,1,0:T(8,128)}), f32[4,128,1024]{2,1,0:T(8,128)S(1)}, u32[]{:S(2)}, u32[]{:S(2)}) %all-to-all-start.3) | async-done | bytes 2097184 | tf_op jit(solution)/shard_map/all_to_all | solution.py:65
  807.1 7.7 all-to-all-start.1
  819.1 2.7 multiply_reduce_fusion
  821.9 37.4 %all-to-all-done.1 = f32[4,128,1024]{2,1,0:T(8,128)} async-done(((f32[4,128,1024]{2,1,0:T(8,128)}), f32[4,128,1024]{2,1,0:T(8,128)}, u32[]{:S(2)}, u32[]{:S(2)}) %all-to-all-start.1) | async-done | bytes 2097184 | tf_op jit(solution)/shard_map/all_to_all | solution.py:65
  859.2 2.8 multiply_reduce_fusion.1
  864.5 3.7 fusion.18
  872.0 41.9 %all-reduce = (f32[2]{0:T(128)S(1)}, f32[2]{0:T(128)S(1)}, f32[2]{0:T(128)S(1)}) all-reduce(f32[2]{0:T(128)S(1)} %pad_maximum_fusion.3, f32[2]{0:T(128)S(1)} %get-tuple-element.20, f32[2]{0:T(128)S(1)} %get-tuple-element.19), channel_id=1, replica_groups=mesh['tok'=8,'col'=4] {'tok','col'}, use_global_device_ids=true, to_apply=%region_10.11 | all-reduce | flops 6 | bytes 48 | tf_op jit(solution)/shard_map/psum | solution.py:73
  (31 shorter events, 14.3 us)
Async XLA Ops:
  7.2 223.1 %all-gather.8.cloned.1.call-start = ((), (), s32[]{:S(2)}) async-start(), calls=%async_computation.9 | async-start | bytes 15728640 | tf_op jit(solution)/shard_map/all_gather | solution.py:40
  13.5 0.8 copy-start.1
  13.5 0.9 copy-start.3
  13.5 435.3 %all-gather.6.cloned.1.call-start = ((), (), s32[]{:S(2)}) async-start(), calls=%async_computation.8 | async-start | bytes 15728640 | tf_op jit(solution)/shard_map/all_gather | solution.py:40
  14.3 555.3 %reduce-scatter.5.cloned.1.call-start = ((), (), s32[]{:S(2)}) async-start(), calls=%async_computation.7 | async-start | bytes 18874368 | tf_op jit(solution)/shard_map/reduce_scatter | solution.py:53
  349.4 339.8 %reduce-scatter.3.cloned.1.call-start = ((), (), s32[]{:S(2)}) async-start(), calls=%async_computation.6 | async-start | bytes 18874368 | tf_op jit(solution)/shard_map/reduce_scatter | solution.py:53
  568.6 0.7 copy-start.2
  586.2 119.3 %all-to-all-start.2 = ((f32[4,128,1024]{2,1,0:T(8,128)}), f32[4,128,1024]{2,1,0:T(8,128)S(1)}, u32[]{:S(2)}, u32[]{:S(2)}) async-start(f32[4,128,1024]{2,1,0:T(8,128)} %bitcast.89), calls=%async_computation.4 | async-start | bytes 4194304 | tf_op jit(solution)/shard_map/all_to_all | solution.py:63
  705.5 50.0 %all-to-all-start = ((f32[4,128,1024]{2,1,0:T(8,128)}), f32[4,128,1024]{2,1,0:T(8,128)}, u32[]{:S(2)}, u32[]{:S(2)}) async-start(f32[4,128,1024]{2,1,0:T(8,128)} %bitcast.88), calls=%async_computation.1 | async-start | bytes 4194304 | tf_op jit(solution)/shard_map/all_to_all | solution.py:63
  755.4 51.6 %all-to-all-start.3 = ((f32[4,128,1024]{2,1,0:T(8,128)}), f32[4,128,1024]{2,1,0:T(8,128)S(1)}, u32[]{:S(2)}, u32[]{:S(2)}) async-start(f32[4,128,1024]{2,1,0:T(8,128)} %copy.26), calls=%async_computation.5 | async-start | bytes 4194304 | tf_op jit(solution)/shard_map/all_to_all | solution.py:65
  769.1 45.6 %copy-start.4 = (s32[2]{0:T(128)S(1)}, s32[2]{0:T(128)}, u32[]{:S(2)}) copy-start(s32[2]{0:T(128)} %param.13) | copy-start | bytes 28
  807.1 11.4 %copy-start = (f32[4,128,1024]{2,1,0:T(8,128)}, f32[4,128,1024]{2,1,0:T(8,128)S(1)}, u32[]{:S(2)}) copy-start(f32[4,128,1024]{2,1,0:T(8,128)S(1)} %all-to-all-done.3) | copy-start | bytes 6291460
  807.1 52.2 %all-to-all-start.1 = ((f32[4,128,1024]{2,1,0:T(8,128)}), f32[4,128,1024]{2,1,0:T(8,128)}, u32[]{:S(2)}, u32[]{:S(2)}) async-start(f32[4,128,1024]{2,1,0:T(8,128)} %copy.22), calls=%async_computation.2 | async-start | bytes 4194304 | tf_op jit(solution)/shard_map/all_to_all | solution.py:65
Sparse Core Ops, SparseCore 0:
  13.6 216.5 all-gather.7
  232.4 216.3 all-gather.5
  452.4 117.1 reduce-scatter.4
  572.9 116.1 reduce-scatter.2
where the time goes:
time: 929 us; the launch traced here: 921 us
  waiting for transfers between devices  514 us (55%)
  matrix products  192 us (21%)
  local copies, waits for them, and re-layouts  103 us (11%)
  blocking collectives  50.8 us (5%)
  starting transfers between devices  27 us (3%)
  between operations  17.9 us (2%)
  other arithmetic  16.1 us (2%)
    all_gather x2, waiting for transfers between devices, body(): lax.all_gather(activations[seq_number], 'col', axis=1, tiled=True)  306 us
    reduce_scatter x2, waiting for transfers between devices, body(): lax.psum_scatter(term_rows(jnp.int32(0), lax.axis_size('tok') * local_row...  96.3 us
    all_to_all x2, waiting for transfers between devices, body(): lax.all_to_all(mixed_cols, 'col', split_axis=0, concat_axis=0, tiled=True)  72.8 us
    dot_general x2, matrix products, body(): blocks = jnp.einsum('rs,asc->arc', rows_table, blocks, precision=HIGH)  68.9 us
    dot_general x2, matrix products, body(): blocks = jnp.einsum('ab,brc->arc', tok_table, blocks, precision=HIGH)  43.2 us
    psum x1, blocking collectives, body(): lax.psum((jnp.stack(crosses), jnp.stack(owns), jnp.stack(refsqs)), ('tok'...  41.9 us
    all_to_all x2, waiting for transfers between devices, body(): lax.all_to_all(pieces, 'col', split_axis=0, concat_axis=0, tiled=True)  38.1 us
    dot_general x2, matrix products, body(): jnp.einsum('tr,tc->rc', features, masked, preferred_element_type=jnp.floa...  36.4 us
  transfers between devices with their start and end apart: 8, of which 7 were waited for; matrix products, arithmetic and copies ran while one was open for 32% of the time, Pallas kernels for 0%

commit v1 on v0

--- a/solution.py
+++ b/solution.py
@@ -6,6 +6,32 @@
 
 D = 4096
 HIGH = lax.Precision.HIGHEST
+
+
+def work_both_ways(shard, axis, dim, work, out_dim):
+    size, place, extent = (lax.axis_size(axis), lax.axis_index(axis), shard.shape[dim])
+    upward = [(i, (i + 1) % size) for i in range(size)]
+    downward = [(b, a) for a, b in upward]
+    lower, upper = (lax.ppermute(shard, axis, upward), lax.ppermute(shard, axis, downward))
+    made = work(shard, place * extent)
+    length = made.shape[out_dim]
+    filled = jnp.zeros(
+        (*made.shape[:out_dim], size * length, *made.shape[out_dim + 1 :]), made.dtype
+    )
+
+    def put(filled, made, source):
+        return lax.dynamic_update_slice_in_dim(filled, made, source * length, axis=out_dim)
+
+    filled = put(filled, made, place)
+    for step in range(1, size // 2 + 1):
+        below, above = ((place - step) % size, (place + step) % size)
+        current = (lower, upper)
+        if step < size // 2:
+            lower, upper = (lax.ppermute(lower, axis, upward), lax.ppermute(upper, axis, downward))
+        filled = put(filled, work(current[0], below * extent), below)
+        if 2 * step < size:
+            filled = put(filled, work(current[1], above * extent), above)
+    return filled
 
 
 def hadamard(order):
@@ -37,10 +63,15 @@
     owns = []
     refsqs = []
     for seq_number in range(activations.shape[0]):
-        features = lax.all_gather(activations[seq_number], "col", axis=1, tiled=True)
         masked = out_grads[seq_number] * token_mask[seq_number][:, None].astype(jnp.bfloat16)
-        partial_value = jnp.einsum(
-            "tr,tc->rc", features, masked, preferred_element_type=jnp.float32
+        partial_value = work_both_ways(
+            activations[seq_number],
+            "col",
+            1,
+            lambda part, at: jnp.einsum(
+                "tr,tc->rc", part, masked, preferred_element_type=jnp.float32
+            ),
+            0,
         )
         blocks = (partial_value * full_pm[:, None]).reshape(tok_count, local_rows, local_cols)
         blocks = jnp.einsum("rs,asc->arc", rows_table, blocks, precision=HIGH)

time: 929 us -> 1050 us (1.13)
  matrix products: 192 us -> 260 us
  waiting for transfers between devices: 514 us -> 538 us
  other arithmetic: 16.1 us -> 34 us
  starting transfers between devices: 27 us -> 37.9 us
    ppermute x0 -> x6, waiting for transfers between devices: none -> 333 us  [the longest x2 233 us: work_both_ways(): lax.ppermute(shard, axis, upward)]
    all_gather x2 -> x0, waiting for transfers between devices: 306 us -> none  [body(): lax.all_gather(activations[seq_number], 'col', axis=1, tiled=True)]
    dot_general x2, matrix products: 68.9 us -> 125 us  [body(): blocks = jnp.einsum('rs,asc->arc', rows_table, blocks, precision=HIGH)]
    mul x0 -> x1, other arithmetic: none -> 17.9 us  [body(): partial_value * full_pm[:, None]]
    dot_general x2 -> x8, matrix products: 36.4 us -> 48.4 us  [body(): jnp.einsum('tr,tc->rc', part, masked, preferred_element_type=jnp.float32)]
    ppermute x0 -> x6, starting transfers between devices: none -> 10.6 us  [the longest x2 4.75 us: work_both_ways(): lax.ppermute(lower, axis, upward)]
    unnamed x12 -> x18, local copies, waits for them, and re-layouts: 21.9 us -> 12.1 us
  transfers between devices with their start and end apart: 8 -> 12, of which waited for: 7 -> 8; matrix products, arithmetic and copies ran while one was open for 32% -> 21% of each run, Pallas kernels for 0% -> 0%
where the time goes in v1:
time: 1050 us; the launch traced here: 1040 us
  waiting for transfers between devices  538 us (51%)
  matrix products  260 us (25%)
  local copies, waits for them, and re-layouts  96.8 us (9%)
  blocking collectives  50.8 us (5%)
  starting transfers between devices  37.9 us (4%)
  other arithmetic  34 us (3%)
  between operations  18.2 us (2%)
    ppermute x2, waiting for transfers between devices, work_both_ways(): lax.ppermute(shard, axis, upward)  233 us
    dot_general x2, matrix products, body(): blocks = jnp.einsum('rs,asc->arc', rows_table, blocks, precision=HIGH)  125 us
    ppermute x2, waiting for transfers between devices, work_both_ways(): lax.ppermute(lower, axis, upward)  100 us
    reduce_scatter x2, waiting for transfers between devices, body(): lax.psum_scatter(term_rows(jnp.int32(0), lax.axis_size('tok') * local_row...  94.5 us
    all_to_all x2, waiting for transfers between devices, body(): lax.all_to_all(mixed_cols, 'col', split_axis=0, concat_axis=0, tiled=True)  72.7 us
    dot_general x8, matrix products, body(): jnp.einsum('tr,tc->rc', part, masked, preferred_element_type=jnp.float32)  48.4 us
    dot_general x2, matrix products, body(): blocks = jnp.einsum('ab,brc->arc', tok_table, blocks, precision=HIGH)  42.8 us
    psum x1, blocking collectives, body(): lax.psum((jnp.stack(crosses), jnp.stack(owns), jnp.stack(refsqs)), ('tok'...  41.8 us
  transfers between devices with their start and end apart: 12, of which 8 were waited for; matrix products, arithmetic and copies ran while one was open for 21% of the time, Pallas kernels for 0%

profile of v1, /device:TPU:10, one launch (start us, length us, event | category | flops | bytes accessed | tf_op | source)
XLA Modules:
  0.0 1035.4 jit_solution(16495557766739570625)
XLA Ops:
  18.3 8.9 all-gather
  29.5 6.4 bitcast_dynamic-update-slice_fusion.3
  35.9 5.7 copy-done.1
  43.7 6.5 bitcast_dynamic-update-slice_fusion.7
  50.3 33.4 %collective-permute-done.3 = bf16[1536,1024]{1,0:T(8,128)(2,1)} collective-permute-done((bf16[1536,1024]{1,0:T(8,128)(2,1)}, bf16[1536,1024]{1,0:T(8,128)(2,1)}, u32[]{:S(2)}, u32[]{:S(2)}) %collective-permute-start.3) | collective-permute-done | bytes 3145760 | tf_op jit(solution)/shard_map/ppermute | solution.py:15
  85.3 199.2 %collective-permute-done = bf16[1536,1024]{1,0:T(8,128)(2,1)} collective-permute-done((bf16[1536,1024]{1,0:T(8,128)(2,1)S(1)}, bf16[1536,1024]{1,0:T(8,128)(2,1)}, u32[]{:S(2)}, u32[]{:S(2)}) %collective-permute-start) | collective-permute-done | bytes 3145760 | tf_op jit(solution)/shard_map/ppermute | solution.py:15
  287.7 8.4 bitcast_dynamic-update-slice_fusion.2
  296.1 5.5 bitcast_dynamic-update-slice_fusion.6
  301.6 7.3 bitcast_dynamic-update-slice_fusion.1
  314.5 38.9 %collective-permute-done.5 = bf16[1536,1024]{1,0:T(8,128)(2,1)S(1)} collective-permute-done((bf16[1536,1024]{1,0:T(8,128)(2,1)}, bf16[1536,1024]{1,0:T(8,128)(2,1)S(1)}, u32[]{:S(2)}, u32[]{:S(2)}) %collective-permute-start.5) | collective-permute-done | bytes 3145760 | tf_op jit(solution)/shard_map/ppermute | solution.py:30
  358.5 61.1 %collective-permute-done.2 = bf16[1536,1024]{1,0:T(8,128)(2,1)S(1)} collective-permute-done((bf16[1536,1024]{1,0:T(8,128)(2,1)}, bf16[1536,1024]{1,0:T(8,128)(2,1)S(1)}, u32[]{:S(2)}, u32[]{:S(2)}) %collective-permute-start.2) | collective-permute-done | bytes 3145760 | tf_op jit(solution)/shard_map/ppermute | solution.py:30
  423.3 5.7 copy-done
  429.0 17.9 %broadcast_multiply_fusion.1 = (f32[4096,1024]{1,0:T(8,128)S(1)}, f32[4096,1024]{1,0:T(8,128)}) fusion(f32[4096,1024]{1,0:T(8,128)} %copy-done, f32[4096]{0:T(1024)S(1)} %bitcast.112, f32[4096,1024]{1,0:T(8,128)} %bitcast_dynamic-update-slice_fusion), kind=kLoop, calls=%fused_computation.3 | loop fusion | flops 8388608 | bytes 67125248 | tf_op jit(solution)/shard_map/mul | solution.py:76
  446.9 63.1 %convolution_bitcast_fusion.1 = f32[8,512,1024]{1,2,0:T(8,128)} fusion(f32[8,512,1024]{2,1,0:T(8,128)S(1)} %bitcast.105), kind=kOutput, calls=%fused_computation.1 | convolution fusion | flops 25780551680 | bytes 33554432 | tf_op jit(solution)/shard_map/rs,asc->arc/dot_general | solution.py:77
  510.0 17.0 %copy.28 = f32[8,512,1024]{2,0,1:T(8,128)} copy(f32[8,512,1024]{1,2,0:T(8,128)} %convolution_bitcast_fusion.1) | data formatting | bytes 33554432 | tf_op jit(solution)/shard_map/rs,asc->arc/transpose | solution.py:77
  526.9 21.3 %fusion.72 = f32[8,512,1024]{2,0,1:T(8,128)} fusion(f32[8,512,1024]{2,0,1:T(8,128)} %copy.28), kind=kOutput, calls=%fused_computation.101 | convolution fusion | flops 402654656 | bytes 33554432 | tf_op jit(solution)/shard_map/ab,brc->arc/dot_general | solution.py:78
  548.3 17.7 %copy.29 = f32[8,512,1024]{2,1,0:T(8,128)} copy(f32[8,512,1024]{2,0,1:T(8,128)} %fusion.72) | data formatting | bytes 33554432 | tf_op jit(solution)/shard_map/ab,brc->arc/dot_general | solution.py:78
  566.0 62.0 %convolution_bitcast_fusion = f32[8,512,1024]{1,2,0:T(8,128)} fusion(f32[8,512,1024]{2,1,0:T(8,128)} %bitcast.104), kind=kOutput, calls=%fused_computation | convolution fusion | flops 25780551680 | bytes 33554432 | tf_op jit(solution)/shard_map/rs,asc->arc/dot_general | solution.py:77
  628.1 17.1 %copy.33 = f32[8,512,1024]{2,0,1:T(8,128)} copy(f32[8,512,1024]{1,2,0:T(8,128)} %convolution_bitcast_fusion) | data formatting | bytes 33554432 | tf_op jit(solution)/shard_map/rs,asc->arc/transpose | solution.py:77
  645.1 21.4 %fusion.70 = f32[8,512,1024]{2,0,1:T(8,128)} fusion(f32[8,512,1024]{2,0,1:T(8,128)} %copy.33), kind=kOutput, calls=%fused_computation.100 | convolution fusion | flops 402654656 | bytes 33554432 | tf_op jit(solution)/shard_map/ab,brc->arc/dot_general | solution.py:78
  666.6 17.9 %copy.34 = f32[8,512,1024]{2,1,0:T(8,128)} copy(f32[8,512,1024]{2,0,1:T(8,128)} %fusion.70) | data formatting | bytes 33554432 | tf_op jit(solution)/shard_map/ab,brc->arc/dot_general | solution.py:78
  685.1 16.3 %fusion.27 = f32[512,1024]{1,0:T(8,128)} fusion(f32[512,1024]{1,0:T(8,128)} %reduce-scatter.3.cloned.1.call-done, f32[1024]{0:T(1024)S(1)} %convert_multiply_fusion), kind=kOutput, calls=%fused_computation.48 | convolution fusion | flops 6489112576 | bytes 4198400 | tf_op jit(solution)/shard_map/dot_general | solution.py:92
  701.5 7.3 all-to-all-start
  708.7 94.5 %reduce-scatter.5.cloned.1.call-done = f32[512,1024]{1,0:T(8,128)} async-done(((f32[4096,1024]{1,0:T(8,128)}), f32[512,1024]{1,0:T(8,128)}) %reduce-scatter.5.cloned.1.call-update) | async-done | bytes 2097168 | tf_op jit(solution)/shard_map/reduce_scatter | solution.py:84
  803.2 16.3 %fusion.24 = f32[512,1024]{1,0:T(8,128)} fusion(f32[512,1024]{1,0:T(8,128)} %reduce-scatter.5.cloned.1.call-done, f32[1024]{0:T(1024)S(1)} %convert_multiply_fusion), kind=kOutput, calls=%fused_computation.46 | convolution fusion | flops 6489112576 | bytes 4198400 | tf_op jit(solution)/shard_map/dot_general | solution.py:92
  831.4 38.1 %all-to-all-done.2 = f32[4,128,1024]{2,1,0:T(8,128)} async-done(((f32[4,128,1024]{2,1,0:T(8,128)}), f32[4,128,1024]{2,1,0:T(8,128)}, u32[]{:S(2)}, u32[]{:S(2)}) %all-to-all-start.2) | async-done | bytes 2097184 | tf_op jit(solution)/shard_map/all_to_all | solution.py:94
  869.4 7.1 all-to-all-start.1
  876.6 6.5 fusion.20
  885.6 35.4 %all-to-all-done.1 = f32[4,128,1024]{2,1,0:T(8,128)S(1)} async-done(((f32[4,128,1024]{2,1,0:T(8,128)}), f32[4,128,1024]{2,1,0:T(8,128)S(1)}, u32[]{:S(2)}, u32[]{:S(2)}) %all-to-all-start.1) | async-done | bytes 2097184 | tf_op jit(solution)/shard_map/all_to_all | solution.py:96
  921.0 7.7 all-to-all-start.3
  935.8 37.3 %all-to-all-done.3 = f32[4,128,1024]{2,1,0:T(8,128)} async-done(((f32[4,128,1024]{2,1,0:T(8,128)}), f32[4,128,1024]{2,1,0:T(8,128)}, u32[]{:S(2)}, u32[]{:S(2)}) %all-to-all-start.3) | async-done | bytes 2097184 | tf_op jit(solution)/shard_map/all_to_all | solution.py:96
  986.0 41.8 %all-reduce = (f32[2]{0:T(128)S(1)}, f32[2]{0:T(128)S(1)}, f32[2]{0:T(128)S(1)}) all-reduce(f32[2]{0:T(128)S(1)} %pad_maximum_fusion.3, f32[2]{0:T(128)S(1)} %get-tuple-element.22, f32[2]{0:T(128)S(1)} %get-tuple-element.21), channel_id=1, replica_groups=mesh['tok'=8,'col'=4] {'tok','col'}, use_global_device_ids=true, to_apply=%region_10.11 | all-reduce | flops 6 | bytes 48 | tf_op jit(solution)/shard_map/psum | solution.py:104
  (53 shorter events, 66.4 us)
Async XLA Ops:
  7.2 11.1 %copy-start.3 = (s32[2,1536]{1,0:T(2,128)S(1)}, s32[2,1536]{1,0:T(2,128)}, u32[]{:S(2)}) copy-start(s32[2,1536]{1,0:T(2,128)} %param.9) | copy-start | bytes 36868
  7.2 11.2 %copy-start.5 = (s32[512]{0:T(512)S(1)}, s32[512]{0:T(512)}, u32[]{:S(2)}) copy-start(s32[512]{0:T(512)} %param.10) | copy-start | bytes 6148
  7.2 677.9 %reduce-scatter.3.cloned.1.call-start = ((), (), s32[]{:S(2)}) async-start(), calls=%async_computation.6 | async-start | bytes 18874368 | tf_op jit(solution)/shard_map/reduce_scatter | solution.py:84
  12.5 71.3 %collective-permute-start.3 = (bf16[1536,1024]{1,0:T(8,128)(2,1)}, bf16[1536,1024]{1,0:T(8,128)(2,1)}, u32[]{:S(2)}, u32[]{:S(2)}) collective-permute-start(bf16[1536,1024]{1,0:T(8,128)(2,1)} %get-tuple-element.12), channel_id=1, source_target_pairs={{0,1},{1,2},{2,3},{3,0},{4,5},{5,6},{6,7},{7,4},{8,9},{9,10},{10,1... | collective-permute-start | bytes 9437192 | tf_op jit(solution)/shard_map/ppermute | solution.py:15
  14.0 270.5 %collective-permute-start = (bf16[1536,1024]{1,0:T(8,128)(2,1)S(1)}, bf16[1536,1024]{1,0:T(8,128)(2,1)}, u32[]{:S(2)}, u32[]{:S(2)}) collective-permute-start(bf16[1536,1024]{1,0:T(8,128)(2,1)S(1)} %get-tuple-element.11), channel_id=1, source_target_pairs={{0,1},{1,2},{2,3},{3,0},{4,5},{5,6},{6,7},{7,4},{8,9},{9,10},{10,1... | collective-permute-start | bytes 9437192 | tf_op jit(solution)/shard_map/ppermute | solution.py:15
  15.6 286.0 %collective-permute-start.4 = (bf16[1536,1024]{1,0:T(8,128)(2,1)}, bf16[1536,1024]{1,0:T(8,128)(2,1)}, u32[]{:S(2)}, u32[]{:S(2)}) collective-permute-start(bf16[1536,1024]{1,0:T(8,128)(2,1)} %get-tuple-element.12), channel_id=1, source_target_pairs={{1,0},{2,1},{3,2},{0,3},{5,4},{6,5},{7,6},{4,7},{9,8},{10,9},{11,1... | collective-permute-start | bytes 9437192 | tf_op jit(solution)/shard_map/ppermute | solution.py:15
  16.1 292.9 %collective-permute-start.1 = (bf16[1536,1024]{1,0:T(8,128)(2,1)S(1)}, bf16[1536,1024]{1,0:T(8,128)(2,1)}, u32[]{:S(2)}, u32[]{:S(2)}) collective-permute-start(bf16[1536,1024]{1,0:T(8,128)(2,1)S(1)} %get-tuple-element.11), channel_id=1, source_target_pairs={{1,0},{2,1},{3,2},{0,3},{5,4},{6,5},{7,6},{4,7},{9,8},{10,9},{11,1... | collective-permute-start | bytes 9437192 | tf_op jit(solution)/shard_map/ppermute | solution.py:15
  35.9 5.7 copy-start.1
  43.7 252.4 %slice-start = ((s8[6291456]{0:T(1024)(128)(4,1)}), s8[4194304]{0:T(1024)(128)(4,1)S(1)}, s32[]{:S(2)}) async-start(s8[6291456]{0:T(1024)(128)(4,1)} %bitcast.114), calls=%async_computation.8 | async-start | bytes 8388608
  50.3 245.9 %slice-start.1 = ((s8[6291456]{0:T(1024)(128)(4,1)}), s8[2097152]{0:T(1024)(128)(4,1)S(1)}, s32[]{:S(2)}) async-start(s8[6291456]{0:T(1024)(128)(4,1)} %bitcast.114), calls=%async_computation.9 | async-start | bytes 4194304
  83.7 269.6 %collective-permute-start.5 = (bf16[1536,1024]{1,0:T(8,128)(2,1)}, bf16[1536,1024]{1,0:T(8,128)(2,1)S(1)}, u32[]{:S(2)}, u32[]{:S(2)}) collective-permute-start(bf16[1536,1024]{1,0:T(8,128)(2,1)} %collective-permute-done.3), channel_id=1, source_target_pairs={{0,1},{1,2},{2,3},{3,0},{4,5},{5,6},{6,7},{7,4},{8,9},{9,10},{10,1... | collective-permute-start | bytes 9437192 | tf_op jit(solution)/shard_map/ppermute | solution.py:30
  284.5 135.1 %collective-permute-start.2 = (bf16[1536,1024]{1,0:T(8,128)(2,1)}, bf16[1536,1024]{1,0:T(8,128)(2,1)S(1)}, u32[]{:S(2)}, u32[]{:S(2)}) collective-permute-start(bf16[1536,1024]{1,0:T(8,128)(2,1)} %collective-permute-done), channel_id=1, source_target_pairs={{0,1},{1,2},{2,3},{3,0},{4,5},{5,6},{6,7},{7,4},{8,9},{9,10},{10,1... | collective-permute-start | bytes 9437192 | tf_op jit(solution)/shard_map/ppermute | solution.py:30
  423.3 5.7 copy-start
  566.0 237.2 %reduce-scatter.5.cloned.1.call-start = ((), (), s32[]{:S(2)}) async-start(), calls=%async_computation.7 | async-start | bytes 18874368 | tf_op jit(solution)/shard_map/reduce_scatter | solution.py:84
  684.4 0.7 copy-start.4
  701.5 118.0 %all-to-all-start = ((f32[4,128,1024]{2,1,0:T(8,128)}), f32[4,128,1024]{2,1,0:T(8,128)S(1)}, u32[]{:S(2)}, u32[]{:S(2)}) async-start(f32[4,128,1024]{2,1,0:T(8,128)} %bitcast.111), calls=%async_computation.1 | async-start | bytes 4194304 | tf_op jit(solution)/shard_map/all_to_all | solution.py:94
  819.5 50.0 %all-to-all-start.2 = ((f32[4,128,1024]{2,1,0:T(8,128)}), f32[4,128,1024]{2,1,0:T(8,128)}, u32[]{:S(2)}, u32[]{:S(2)}) async-start(f32[4,128,1024]{2,1,0:T(8,128)} %bitcast.110), calls=%async_computation.4 | async-start | bytes 4194304 | tf_op jit(solution)/shard_map/all_to_all | solution.py:94
  869.4 51.6 %all-to-all-start.1 = ((f32[4,128,1024]{2,1,0:T(8,128)}), f32[4,128,1024]{2,1,0:T(8,128)S(1)}, u32[]{:S(2)}, u32[]{:S(2)}) async-start(f32[4,128,1024]{2,1,0:T(8,128)} %copy.31), calls=%async_computation.2 | async-start | bytes 4194304 | tf_op jit(solution)/shard_map/all_to_all | solution.py:96
  883.1 45.6 %copy-start.6 = (s32[2]{0:T(128)S(1)}, s32[2]{0:T(128)}, u32[]{:S(2)}) copy-start(s32[2]{0:T(128)} %param.13) | copy-start | bytes 28
  921.0 11.4 %copy-start.2 = (f32[4,128,1024]{2,1,0:T(8,128)}, f32[4,128,1024]{2,1,0:T(8,128)S(1)}, u32[]{:S(2)}) copy-start(f32[4,128,1024]{2,1,0:T(8,128)S(1)} %all-to-all-done.1) | copy-start | bytes 6291460
  921.0 52.2 %all-to-all-start.3 = ((f32[4,128,1024]{2,1,0:T(8,128)}), f32[4,128,1024]{2,1,0:T(8,128)}, u32[]{:S(2)}, u32[]{:S(2)}) async-start(f32[4,128,1024]{2,1,0:T(8,128)} %copy.36), calls=%async_computation.5 | async-start | bytes 4194304 | tf_op jit(solution)/shard_map/all_to_all | solution.py:96
Sparse Core Ops, SparseCore 0:
  566.1 117.2 reduce-scatter.2
  687.0 116.1 reduce-scatter.4
